TPU v7x, 512 devices: a whole 4x8x8 slice. The times are simulated.
512 devices in a mesh: grp: 8 (over x, core), ep: 64 (over z, y).
Axes of the slice: x: 4, y: 8, z: 8, core: 2. Of those that a mesh axis runs over, the one named last changes fastest.
Arguments:
- resid: bfloat16 [8192, 2048], P('ep', 'grp'), may hold values from -6 to 6
- query: bfloat16 [8192, 2048], P('ep', 'grp'), may hold values from -6 to 6
- key_new: bfloat16 [8192, 2048], P('ep', 'grp'), may hold values from -6 to 6
- value_new: bfloat16 [8192, 2048], P('ep', 'grp'), may hold values from -6 to 6
- cache_kv: bfloat16 [2, 65536, 2048], P(None, 'ep', 'grp'), may hold values from -6 to 6
- cache_len: int32 [64], replicated, may hold values from 1 to 1024, 16384 in all
- w_out: bfloat16 [2048, 2048], P('grp'), may hold values from -0.125 to 0.125
- norm_gain: bfloat16 [2048], replicated, may hold values from 0.099609375 to 1.8984375
- w_router: bfloat16 [2048, 64], replicated, may hold values from -7 to 7
- routes: int32 [8192, 4], P('ep'), may hold values from 0 to 63, all different within a row; in each aligned block of 128 rows (0 to 127, 128 to 255, ...) at most 16 rows name the same one
- w_gate_up: bfloat16 [64, 2, 2048, 1408], P('ep', None, None, 'grp'), may hold values from -0.125 to 0.125
- w_down: bfloat16 [64, 1408, 2048], P('ep', 'grp'), may hold values from -0.15625 to 0.15625
Outputs:
- after_attention: bfloat16 [8192, 2048], P('ep', 'grp')
- expert_mix: bfloat16 [8192, 2048], P('ep', 'grp')
Inputs may be any that keep to these rules, and one draw needn't show every extreme that they name: `routes`: in each aligned block of 128 rows (one request's tokens), no expert is named by more than 16 of the pairs, and in every draw some expert is named by exactly 16. Request r's cache fills the first cache_len[r] rows of its slab, rows r * 1024 onward of cache_kv; the rest of the slab is unused; the lengths sum to 16384 and the longest is exactly 1024.
All inputs are finite; a program needn't handle non-finite values.
Results may differ from a plain program's by a relative error of at most 0.013.
Values may be sent and summed in bfloat16 or wider, within the bound.
No kernel may reach another device: no remote copies, remote signals or barrier semaphores. Data moves between devices by JAX's collectives and lax.ppermute only.
A program may use at most 64 MiB of HBM per device.

v0:
```python
import jax
import jax.numpy as jnp
from jax import lax
from jax.sharding import PartitionSpec as P

D = 2048
HD = 128
TOP = 4
EPS = 1e-06
MASKED = -1e30


def body(
    resid,
    query,
    key_new,
    value_new,
    cache_kv,
    cache_len,
    w_out,
    norm_gain,
    w_router,
    routes,
    w_gate_up,
    w_down,
):
    tokens_here = query.shape[0]
    heads_here = query.shape[1] // HD
    experts_all = w_router.shape[1]
    column_width = resid.shape[1]
    group_index = lax.axis_index("grp")
    request = lax.axis_index("ep")
    capacity = max(2, 8 * tokens_here // lax.axis_size("ep"))
    score_scale = float(HD) ** (-0.5)
    column_start = group_index * column_width
    queries = query.reshape(tokens_here, heads_here, HD)
    new_keys = key_new.reshape(tokens_here, heads_here, HD)
    new_values = value_new.reshape(tokens_here, heads_here, HD)
    cache_rows = cache_kv.shape[1]
    cache_keys = cache_kv[0].reshape(cache_rows, heads_here, HD)
    cache_values = cache_kv[1].reshape(cache_rows, heads_here, HD)
    own_length = lax.dynamic_index_in_dim(cache_len, request, 0, keepdims=False)
    position = jnp.arange(tokens_here, dtype=jnp.int32)
    causal = (position[:, None] >= position[None, :])[:, None, :]
    new_scores = (
        jnp.einsum("qhd,khd->qhk", queries, new_keys, preferred_element_type=jnp.float32)
        * score_scale
    )
    new_scores = jnp.where(causal, new_scores, MASKED)
    live_rows = (jnp.arange(cache_rows, dtype=jnp.int32) < own_length)[None, None, :]
    old_scores = (
        jnp.einsum("qhd,khd->qhk", queries, cache_keys, preferred_element_type=jnp.float32)
        * score_scale
    )
    old_scores = jnp.where(live_rows, old_scores, MASKED)
    row_max = jnp.maximum(jnp.max(new_scores, axis=-1), jnp.max(old_scores, axis=-1))
    new_probs = jnp.exp(new_scores - row_max[..., None])
    old_probs = jnp.exp(old_scores - row_max[..., None])
    denominator = jnp.sum(new_probs, axis=-1) + jnp.sum(old_probs, axis=-1)
    weighted = jnp.einsum(
        "qhk,khd->qhd",
        new_probs.astype(jnp.bfloat16),
        new_values,
        preferred_element_type=jnp.float32,
    )
    weighted = weighted + jnp.einsum(
        "qhk,khd->qhd",
        old_probs.astype(jnp.bfloat16),
        cache_values,
        preferred_element_type=jnp.float32,
    )
    attended = (
        (weighted / denominator[..., None])
        .astype(jnp.bfloat16)
        .reshape(tokens_here, heads_here * HD)
    )
    projected = jnp.dot(attended, w_out, preferred_element_type=jnp.float32)
    attn_share = lax.psum_scatter(projected, "grp", scatter_dimension=1, tiled=True)
    after_cols = (resid.astype(jnp.float32) + attn_share).astype(jnp.bfloat16)
    after_full = lax.all_gather(after_cols, "grp", axis=1, tiled=True)
    after_wide = after_full.astype(jnp.float32)
    squares = jnp.sum(after_wide * after_wide, axis=1)
    inverse = lax.rsqrt(squares / D + EPS)
    normed_full = (after_wide * inverse[:, None] * norm_gain.astype(jnp.float32)[None, :]).astype(
        jnp.bfloat16
    )
    normed_cols = lax.dynamic_slice_in_dim(normed_full, column_start, column_width, 1)
    logits = jnp.dot(normed_full, w_router, preferred_element_type=jnp.float32)
    route_hits = routes[:, :, None] == jnp.arange(experts_all, dtype=jnp.int32)[None, None, :]
    chosen = jnp.sum(jnp.where(route_hits, logits[:, None, :], 0.0), axis=-1)
    route_weight = jax.nn.softmax(chosen, axis=-1).astype(jnp.bfloat16)
    flat_hits = route_hits.reshape(tokens_here * TOP, experts_all).astype(jnp.int32)
    earlier = jnp.cumsum(flat_hits, axis=0) - flat_hits
    slot_index = jnp.sum(earlier * flat_hits, axis=1)
    slot_row = (routes.reshape(-1) * capacity + slot_index).reshape(tokens_here, TOP)
    slot_ids = jnp.arange(experts_all * capacity, dtype=jnp.int32)
    matches = slot_row[:, :, None] == slot_ids[None, None, :]
    selection = jnp.any(matches, axis=1).astype(jnp.bfloat16)
    combine = jnp.sum(jnp.where(matches, route_weight[:, :, None].astype(jnp.float32), 0.0), axis=1)
    outgoing = jnp.einsum(
        "tj,td->jd", selection, normed_cols, preferred_element_type=jnp.float32
    ).astype(jnp.bfloat16)
    outgoing = outgoing.reshape(experts_all, capacity, column_width)
    arrived = lax.all_to_all(outgoing, "ep", split_axis=0, concat_axis=0, tiled=True)
    arrived = arrived.reshape(experts_all * capacity, column_width)
    groups = lax.axis_size("grp")
    gathered = lax.all_gather(arrived, "grp", axis=0, tiled=False)
    slice_width = w_gate_up.shape[-1]
    gate_up = w_gate_up[0].reshape(2, groups, column_width, slice_width)
    gate_value = jnp.einsum("gnc,gch->nh", gathered, gate_up[0], preferred_element_type=jnp.float32)
    up_value = jnp.einsum("gnc,gch->nh", gathered, gate_up[1], preferred_element_type=jnp.float32)
    hidden = (jax.nn.silu(gate_value) * up_value).astype(jnp.bfloat16)
    down = w_down[0].reshape(slice_width, groups, column_width)
    slice_out = jnp.einsum("nh,hgc->gnc", hidden, down, preferred_element_type=jnp.float32).astype(
        jnp.bfloat16
    )
    slices_here = lax.all_to_all(slice_out, "grp", split_axis=0, concat_axis=0, tiled=True)
    expert_out = jnp.sum(slices_here.astype(jnp.float32), axis=0)
    expert_out = expert_out.reshape(experts_all, capacity, column_width)
    returned = lax.all_to_all(expert_out, "ep", split_axis=0, concat_axis=0, tiled=True)
    mixed_cols = jnp.dot(
        combine,
        returned.reshape(experts_all * capacity, column_width),
        precision=lax.Precision.HIGHEST,
        preferred_element_type=jnp.float32,
    )
    return (after_cols, mixed_cols.astype(jnp.bfloat16))


def solution(mesh):
    return jax.shard_map(
        body,
        mesh=mesh,
        in_specs=(
            P("ep", "grp"),
            P("ep", "grp"),
            P("ep", "grp"),
            P("ep", "grp"),
            P(None, "ep", "grp"),
            P(),
            P("grp", None),
            P(),
            P(),
            P("ep", None),
            P("ep", None, None, "grp"),
            P("ep", "grp", None),
        ),
        out_specs=(P("ep", "grp"), P("ep", "grp")),
        check_vma=False,
    )
```

profile of v0, /device:TPU:8, one launch (start us, length us, event | category | flops | bytes accessed | tf_op | source)
XLA Modules:
  0.0 251.8 jit_solution(18026099072781676729)
XLA Ops:
  7.3 1.3 dynamic_slice.7
  8.6 0.6 iota_compare_fusion.5
  9.3 1.0 copy.117
  10.2 1.3 fusion.49
  11.5 0.2 copy.105
  11.7 0.2 copy.118
  11.9 0.2 fusion.50
  12.1 0.4 fusion.51
  13.0 0.3 fusion.10
  13.3 1.3 fusion.52
  15.1 1.2 reduce-window.6
  16.3 0.2 slice_reduce_fusion
  16.9 0.4 fusion
  17.3 39.2 %reduce-scatter.2.cloned.1.call-done = f32[128,256]{1,0:T(8,128)} async-done(((f32[128,2048]{1,0:T(8,128)}), f32[128,256]{1,0:T(8,128)}) %reduce-scatter.2.cloned.1.call-update) | async-done | bytes 131088 | tf_op jit(solution)/shard_map/reduce_scatter | solution.py:78
  56.5 0.9 add_convert_fusion
  57.5 13.1 %all_gather.6 = bf16[128,2048]{1,0:T(8,128)(2,1)S(1)} all-gather(bf16[128,256]{1,0:T(8,128)(2,1)S(1)} %add_convert_fusion), channel_id=1, replica_groups=mesh['grp'=8,'ep'=64] {'grp'}, dimensions={1}, use_global_device_ids=true | all-gather | bytes 589824 | tf_op jit(solution)/shard_map/all_gather | solution.py:80
  70.6 0.2 fusion.11
  70.8 0.2 fusion.13
  71.0 0.4 convolution_convert_fusion
  71.3 33.1 %all_to_all.15 = bf16[64,16,256]{2,1,0:T(8,128)(2,1)} all-to-all(bf16[64,16,256]{2,1,0:T(8,128)(2,1)S(1)} %bitcast.115), channel_id=1, replica_groups=mesh['grp'=8,'ep'=64] {'ep'}, dimensions={0} | all-to-all | bytes 1048576 | tf_op jit(solution)/shard_map/all_to_all | solution.py:104
  104.5 2.2 copy.124
  106.7 1.0 copy.122
  108.0 26.0 %all-gather.2.cloned.1.call-done = bf16[8,1024,256]{2,1,0:T(8,128)(2,1)} async-done(((bf16[1,1024,256]{2,1,0:T(8,128)(2,1)}), bf16[8,1024,256]{2,1,0:T(8,128)(2,1)}) %all-gather.2.cloned.1.call-update) | async-done | bytes 4194320 | tf_op jit(solution)/shard_map/all_gather | solution.py:107
  133.9 4.8 %convolution_bitcast_fusion.1 = f32[1024,176]{0,1:T(8,128)} fusion(bf16[8,1024,256]{2,1,0:T(8,128)(2,1)} %all-gather.2.cloned.1.call-done, bf16[8,256,176]{1,0,2:T(8,128)(2,1)} %bitcast.120), kind=kOutput, calls=%fused_computation.12 | convolution fusion | flops 738197504 | bytes 5636096 | tf_op jit(solution)/shard_map/gnc,gch->nh/dot_general | solution.py:110
  138.8 7.1 %convert_bitcast_fusion = bf16[8,1024,256]{2,1,0:T(8,128)(2,1)} fusion(bf16[8,1024,256]{2,1,0:T(8,128)(2,1)} %all-gather.2.cloned.1.call-done, bf16[176,8,256]{2,1,0:T(8,128)(2,1)S(1)} %bitcast.118, bf16[8,256,176]{1,0,2:T(8,128)(2,1)S(1)} %bitcast.119, f32[1024,176]{0,1:T(8,128)} %convolution_bitcast_fusion.1), kind=kOutput, calls=%fused_computation.1 | convolution fusion | flops 1479573504 | bytes 10551296 | tf_op jit(solution)/shard_map/nh,hgc->gnc/dot_general | solution.py:114
  145.8 53.9 %all_to_all.16 = bf16[8,1024,256]{2,1,0:T(8,128)(2,1)S(1)} all-to-all(bf16[8,1024,256]{2,1,0:T(8,128)(2,1)} %convert_bitcast_fusion), channel_id=1, replica_groups=mesh['grp'=8,'ep'=64] {'grp'}, dimensions={0} | all-to-all | bytes 8388608 | tf_op jit(solution)/shard_map/all_to_all | solution.py:117
  199.7 1.6 convert_reduce_fusion
  201.3 13.4 %all-to-all-start.2 = ((f32[64,16,256]{2,1,0:T(8,128)}), f32[64,16,256]{2,1,0:T(8,128)S(1)}, u32[]{:S(2)}, u32[]{:S(2)}) async-start(f32[64,16,256]{2,1,0:T(8,128)} %bitcast.15), calls=%async_computation.3 | async-start | bytes 2097152 | tf_op jit(solution)/shard_map/all_to_all | solution.py:120
  214.7 0.3 fusion.53
  215.1 0.3 select_reduce_fusion
  215.4 28.2 %all-to-all-done.2 = f32[64,16,256]{2,1,0:T(8,128)S(1)} async-done(((f32[64,16,256]{2,1,0:T(8,128)}), f32[64,16,256]{2,1,0:T(8,128)S(1)}, u32[]{:S(2)}, u32[]{:S(2)}) %all-to-all-start.2) | async-done | bytes 1048608 | tf_op jit(solution)/shard_map/all_to_all | solution.py:120
  243.6 1.3 convolution_convert_fusion.1
  (48 shorter events, 1.6 us)
Async XLA Ops:
  7.2 6.2 %copy-start = (bf16[256,2048]{1,0:T(8,128)(2,1)S(1)}, bf16[256,2048]{1,0:T(8,128)(2,1)}, u32[]{:S(2)}) copy-start(bf16[256,2048]{1,0:T(8,128)(2,1)} %param.18) | copy-start | bytes 3145732
  7.2 4.7 %copy-start.5 = (bf16[128,256]{1,0:T(8,128)(2,1)S(1)}, bf16[128,256]{1,0:T(8,128)(2,1)}, u32[]{:S(2)}) copy-start(bf16[128,256]{1,0:T(8,128)(2,1)} %param.13) | copy-start | bytes 196612
  7.2 4.7 %copy-start.9 = (bf16[128,256]{1,0:T(8,128)(2,1)S(1)}, bf16[128,256]{1,0:T(8,128)(2,1)}, u32[]{:S(2)}) copy-start(bf16[128,256]{1,0:T(8,128)(2,1)} %param.14) | copy-start | bytes 196612
  7.2 49.3 %reduce-scatter.2.cloned.1.call-start = ((), (), s32[]{:S(2)}) async-start(), calls=%async_computation.4 | async-start | bytes 1179648 | tf_op jit(solution)/shard_map/reduce_scatter | solution.py:78
  11.9 2.8 %copy-start.7 = (s32[128,4]{0,1:T(4,128)S(1)}, s32[128,4]{0,1:T(4,128)}, u32[]{:S(2)}) copy-start(s32[128,4]{0,1:T(4,128)} %param.21) | copy-start | bytes 6148
  12.1 2.9 %copy-start.8 = (bf16[2048]{0:T(1024)(128)(2,1)S(1)}, bf16[2048]{0:T(1024)(128)(2,1)}, u32[]{:S(2)}) copy-start(bf16[2048]{0:T(1024)(128)(2,1)} %param.19) | copy-start | bytes 12292
  12.6 44.0 %copy-start.6 = (bf16[128,256]{1,0:T(8,128)(2,1)S(1)}, bf16[128,256]{1,0:T(8,128)(2,1)}, u32[]{:S(2)}) copy-start(bf16[128,256]{1,0:T(8,128)(2,1)} %param.12) | copy-start | bytes 196612
  14.7 92.0 %copy-start.1 = (bf16[1,2,2048,176]{2,3,1,0:T(8,128)(2,1)S(1)}, bf16[1,2,2048,176]{2,3,1,0:T(8,128)(2,1)}, u32[]{:S(2)}) copy-start(bf16[1,2,2048,176]{2,3,1,0:T(8,128)(2,1)} %param.22) | copy-start | bytes 4325380
  14.7 119.3 %all-gather.2.cloned.1.call-start = ((), (), s32[]{:S(2)}) async-start(), calls=%async_computation.5 | async-start | bytes 4718592 | tf_op jit(solution)/shard_map/all_gather | solution.py:107
  57.5 49.3 %copy-start.4 = (bf16[128,256]{1,0:T(8,128)(2,1)}, bf16[128,256]{1,0:T(8,128)(2,1)S(1)}, u32[]{:S(2)}) copy-start(bf16[128,256]{1,0:T(8,128)(2,1)S(1)} %add_convert_fusion) | copy-start | bytes 196612
  107.8 31.0 %copy-start.2 = (bf16[22,8,8,256]{3,2,1,0:T(8,128)(2,1)S(1)}, bf16[22,8,8,256]{3,2,1,0:T(8,128)(2,1)}, u32[]{:S(2)}) copy-start(bf16[22,8,8,256]{3,2,1,0:T(8,128)(2,1)} %copy.124) | copy-start | bytes 2162692
  199.7 15.0 %copy-start.3 = (bf16[2048,64]{0,1:T(8,128)(2,1)S(1)}, bf16[2048,64]{0,1:T(8,128)(2,1)}, u32[]{:S(2)}) copy-start(bf16[2048,64]{0,1:T(8,128)(2,1)} %param.20) | copy-start | bytes 786436
  201.3 42.3 %all-to-all-start.2 = ((f32[64,16,256]{2,1,0:T(8,128)}), f32[64,16,256]{2,1,0:T(8,128)S(1)}, u32[]{:S(2)}, u32[]{:S(2)}) async-start(f32[64,16,256]{2,1,0:T(8,128)} %bitcast.15), calls=%async_computation.3 | async-start | bytes 2097152 | tf_op jit(solution)/shard_map/all_to_all | solution.py:120
Sparse Core Ops, SparseCore 0:
  14.8 41.6 reduce-scatter.1
  104.6 29.3 all-gather.1
where the time goes:
time: 252 us
  blocking collectives  100 us (40%)
  waiting for transfers between devices  93.5 us (37%)
  matrix products  16.2 us (6%)
  between operations  14.3 us (6%)
  starting transfers between devices  13.5 us (5%)
  local copies, waits for them, and re-layouts  8.21 us (3%)
  other arithmetic  5.93 us (2%)
    all_to_all x1, blocking collectives, body(): lax.all_to_all(slice_out, 'grp', split_axis=0, concat_axis=0, tiled=True)  53.9 us
    reduce_scatter x1, waiting for transfers between devices, body(): lax.psum_scatter(projected, 'grp', scatter_dimension=1, tiled=True)  39.2 us
    all_to_all x1, blocking collectives, body(): lax.all_to_all(outgoing, 'ep', split_axis=0, concat_axis=0, tiled=True)  33.1 us
    all_to_all x1, waiting for transfers between devices, body(): lax.all_to_all(expert_out, 'ep', split_axis=0, concat_axis=0, tiled=True)  28.2 us
    all_gather x1, waiting for transfers between devices, body(): gathered = lax.all_gather(arrived, 'grp', axis=0, tiled=False)  26 us
    all_to_all x1, starting transfers between devices, body(): lax.all_to_all(expert_out, 'ep', split_axis=0, concat_axis=0, tiled=True)  13.4 us
    all_gather x1, blocking collectives, body(): after_full = lax.all_gather(after_cols, 'grp', axis=1, tiled=True)  13.1 us
    dot_general x1, matrix products, body(): jnp.einsum('nh,hgc->gnc', hidden, down, preferred_element_type=jnp.float32)  7.06 us
  transfers between devices with their start and end apart: 3, of which 3 were waited for; matrix products, arithmetic and copies ran while one was open for 3% of the time, Pallas kernels for 0%

commit v1 on v0

--- a/solution.py
+++ b/solution.py
@@ -77,7 +77,9 @@
     projected = jnp.dot(attended, w_out, preferred_element_type=jnp.float32)
     attn_share = lax.psum_scatter(projected, "grp", scatter_dimension=1, tiled=True)
     after_cols = (resid.astype(jnp.float32) + attn_share).astype(jnp.bfloat16)
-    after_full = lax.all_gather(after_cols, "grp", axis=1, tiled=True)
+    after_full = jnp.concatenate(
+        lax.all_to_all(jnp.stack([after_cols] * lax.axis_size("grp")), "grp", 0, 0), axis=1
+    )
     after_wide = after_full.astype(jnp.float32)
     squares = jnp.sum(after_wide * after_wide, axis=1)
     inverse = lax.rsqrt(squares / D + EPS)

time: 252 us -> 254 us (level)
  blocking collectives: 100 us -> 86.5 us
  waiting for transfers between devices: 93.5 us -> 103 us
  starting transfers between devices: 13.5 us -> 16.9 us
    all_gather x1 -> x0, blocking collectives: 13.1 us -> none  [body(): after_full = lax.all_gather(after_cols, 'grp', axis=1, tiled=True)]
    all_to_all x0 -> x1, waiting for transfers between devices: none -> 8.84 us  [body(): lax.all_to_all(jnp.stack([after_cols] * lax.axis_size('grp')), 'grp', 0, 0)]
    all_to_all x0 -> x1, starting transfers between devices: none -> 3.49 us  [body(): lax.all_to_all(jnp.stack([after_cols] * lax.axis_size('grp')), 'grp', 0, 0)]
  transfers between devices with their start and end apart: 3 -> 4, of which waited for: 3 -> 4; matrix products, arithmetic and copies ran while one was open for 3% -> 3% of each run, Pallas kernels for 0% -> 0%
where the time goes in v1:
time: 254 us; the launch traced here: 253 us
  waiting for transfers between devices  103 us (41%)
  blocking collectives  86.5 us (34%)
  matrix products  17 us (7%)
  starting transfers between devices  16.9 us (7%)
  between operations  14.3 us (6%)
  local copies, waits for them, and re-layouts  9.18 us (4%)
  other arithmetic  6.83 us (3%)
    all_to_all x1, blocking collectives, body(): lax.all_to_all(slice_out, 'grp', split_axis=0, concat_axis=0, tiled=True)  53.9 us
    reduce_scatter x1, waiting for transfers between devices, body(): lax.psum_scatter(projected, 'grp', scatter_dimension=1, tiled=True)  40 us
    all_to_all x1, blocking collectives, body(): lax.all_to_all(outgoing, 'ep', split_axis=0, concat_axis=0, tiled=True)  32.5 us
    all_to_all x1, waiting for transfers between devices, body(): lax.all_to_all(expert_out, 'ep', split_axis=0, concat_axis=0, tiled=True)  28.3 us
    all_gather x1, waiting for transfers between devices, body(): gathered = lax.all_gather(arrived, 'grp', axis=0, tiled=False)  25.5 us
    all_to_all x1, starting transfers between devices, body(): lax.all_to_all(expert_out, 'ep', split_axis=0, concat_axis=0, tiled=True)  13.4 us
    all_to_all x1, waiting for transfers between devices, body(): lax.all_to_all(jnp.stack([after_cols] * lax.axis_size('grp')), 'grp', 0, 0)  8.84 us
    dot_general x1, matrix products, body(): jnp.einsum('nh,hgc->gnc', hidden, down, preferred_element_type=jnp.float32)  7.06 us
  transfers between devices with their start and end apart: 4, of which 4 were waited for; matrix products, arithmetic and copies ran while one was open for 3% of the time, Pallas kernels for 0%

profile of v1, /device:TPU:8, one launch (start us, length us, event | category | flops | bytes accessed | tf_op | source)
XLA Modules:
  0.0 253.5 jit_solution(11696466680993686815)
XLA Ops:
  7.3 1.3 dynamic_slice.7
  8.6 0.6 iota_compare_fusion.5
  9.3 1.0 copy.122
  10.2 1.3 fusion.49
  11.5 0.2 copy.109
  12.2 0.4 fusion.51
  13.0 0.3 fusion.10
  13.3 1.3 fusion.52
  15.1 1.2 reduce-window.6
  16.3 0.2 slice_reduce_fusion
  16.5 40.0 %reduce-scatter.2.cloned.1.call-done = f32[128,256]{1,0:T(8,128)} async-done(((f32[128,2048]{1,0:T(8,128)}), f32[128,256]{1,0:T(8,128)}) %reduce-scatter.2.cloned.1.call-update) | async-done | bytes 131088 | tf_op jit(solution)/shard_map/reduce_scatter | solution.py:78
  56.5 0.9 add_convert_fusion
  57.6 0.9 stack.2
  58.4 3.5 %all-to-all-start = ((bf16[8,128,256]{1,2,0:T(8,128)(2,1)}), bf16[8,128,256]{1,2,0:T(8,128)(2,1)S(1)}, u32[]{:S(2)}, u32[]{:S(2)}) async-start(bf16[8,128,256]{1,2,0:T(8,128)(2,1)} %stack.2), calls=%async_computation.1 | async-start | bytes 1048576 | tf_op jit(solution)/shard_map/all_to_all | solution.py:81
  62.3 1.1 fusion
  63.4 8.8 %all-to-all-done = bf16[8,128,256]{1,2,0:T(8,128)(2,1)S(1)} async-done(((bf16[8,128,256]{1,2,0:T(8,128)(2,1)}), bf16[8,128,256]{1,2,0:T(8,128)(2,1)S(1)}, u32[]{:S(2)}, u32[]{:S(2)}) %all-to-all-start) | async-done | bytes 524320 | tf_op jit(solution)/shard_map/all_to_all | solution.py:81
  72.2 0.3 multiply_reduce_fusion
  72.5 0.3 fusion.12
  72.8 1.2 convolution_convert_fusion
  74.1 32.5 %all_to_all.20 = bf16[64,16,256]{2,1,0:T(8,128)(2,1)} all-to-all(bf16[64,16,256]{2,1,0:T(8,128)(2,1)S(1)} %bitcast.122), channel_id=1, replica_groups=mesh['grp'=8,'ep'=64] {'ep'}, dimensions={0} | all-to-all | bytes 1048576 | tf_op jit(solution)/shard_map/all_to_all | solution.py:106
  106.7 2.2 copy.129
  108.9 1.0 copy.127
  110.2 25.5 %all-gather.2.cloned.1.call-done = bf16[8,1024,256]{2,1,0:T(8,128)(2,1)} async-done(((bf16[1,1024,256]{2,1,0:T(8,128)(2,1)}), bf16[8,1024,256]{2,1,0:T(8,128)(2,1)}) %all-gather.2.cloned.1.call-update) | async-done | bytes 4194320 | tf_op jit(solution)/shard_map/all_gather | solution.py:109
  135.6 4.8 %convolution_bitcast_fusion.1 = f32[1024,176]{0,1:T(8,128)} fusion(bf16[8,1024,256]{2,1,0:T(8,128)(2,1)} %all-gather.2.cloned.1.call-done, bf16[8,256,176]{1,0,2:T(8,128)(2,1)} %bitcast.127), kind=kOutput, calls=%fused_computation.10 | convolution fusion | flops 738197504 | bytes 5636096 | tf_op jit(solution)/shard_map/gnc,gch->nh/dot_general | solution.py:112
  140.5 7.1 %convert_bitcast_fusion = bf16[8,1024,256]{2,1,0:T(8,128)(2,1)} fusion(bf16[8,1024,256]{2,1,0:T(8,128)(2,1)} %all-gather.2.cloned.1.call-done, bf16[176,8,256]{2,1,0:T(8,128)(2,1)S(1)} %bitcast.125, bf16[8,256,176]{1,0,2:T(8,128)(2,1)S(1)} %bitcast.126, f32[1024,176]{0,1:T(8,128)} %convolution_bitcast_fusion.1), kind=kOutput, calls=%fused_computation.1 | convolution fusion | flops 1479573504 | bytes 10551296 | tf_op jit(solution)/shard_map/nh,hgc->gnc/dot_general | solution.py:116
  147.5 53.9 %all_to_all.21 = bf16[8,1024,256]{2,1,0:T(8,128)(2,1)S(1)} all-to-all(bf16[8,1024,256]{2,1,0:T(8,128)(2,1)} %convert_bitcast_fusion), channel_id=1, replica_groups=mesh['grp'=8,'ep'=64] {'grp'}, dimensions={0} | all-to-all | bytes 8388608 | tf_op jit(solution)/shard_map/all_to_all | solution.py:119
  201.4 1.6 convert_reduce_fusion
  203.0 13.4 %all-to-all-start.3 = ((f32[64,16,256]{2,1,0:T(8,128)}), f32[64,16,256]{2,1,0:T(8,128)S(1)}, u32[]{:S(2)}, u32[]{:S(2)}) async-start(f32[64,16,256]{2,1,0:T(8,128)} %bitcast.17), calls=%async_computation.4 | async-start | bytes 2097152 | tf_op jit(solution)/shard_map/all_to_all | solution.py:122
  216.4 0.2 fusion.53
  216.7 0.3 select_reduce_fusion
  217.0 28.3 %all-to-all-done.3 = f32[64,16,256]{2,1,0:T(8,128)S(1)} async-done(((f32[64,16,256]{2,1,0:T(8,128)}), f32[64,16,256]{2,1,0:T(8,128)S(1)}, u32[]{:S(2)}, u32[]{:S(2)}) %all-to-all-start.3) | async-done | bytes 1048608 | tf_op jit(solution)/shard_map/all_to_all | solution.py:122
  245.3 1.3 convolution_convert_fusion.1
  (51 shorter events, 2.1 us)
Async XLA Ops:
  7.2 6.2 %copy-start = (bf16[256,2048]{1,0:T(8,128)(2,1)S(1)}, bf16[256,2048]{1,0:T(8,128)(2,1)}, u32[]{:S(2)}) copy-start(bf16[256,2048]{1,0:T(8,128)(2,1)} %param.18) | copy-start | bytes 3145732
  7.2 4.7 %copy-start.5 = (bf16[128,256]{1,0:T(8,128)(2,1)S(1)}, bf16[128,256]{1,0:T(8,128)(2,1)}, u32[]{:S(2)}) copy-start(bf16[128,256]{1,0:T(8,128)(2,1)} %param.13) | copy-start | bytes 196612
  7.2 4.7 %copy-start.9 = (bf16[128,256]{1,0:T(8,128)(2,1)S(1)}, bf16[128,256]{1,0:T(8,128)(2,1)}, u32[]{:S(2)}) copy-start(bf16[128,256]{1,0:T(8,128)(2,1)} %param.14) | copy-start | bytes 196612
  7.2 49.3 %reduce-scatter.2.cloned.1.call-start = ((), (), s32[]{:S(2)}) async-start(), calls=%async_computation.5 | async-start | bytes 1179648 | tf_op jit(solution)/shard_map/reduce_scatter | solution.py:78
  11.9 2.7 %copy-start.7 = (s32[128,4]{0,1:T(4,128)S(1)}, s32[128,4]{0,1:T(4,128)}, u32[]{:S(2)}) copy-start(s32[128,4]{0,1:T(4,128)} %param.21) | copy-start | bytes 6148
  12.1 2.9 %copy-start.8 = (bf16[2048]{0:T(1024)(128)(2,1)S(1)}, bf16[2048]{0:T(1024)(128)(2,1)}, u32[]{:S(2)}) copy-start(bf16[2048]{0:T(1024)(128)(2,1)} %param.19) | copy-start | bytes 12292
  12.1 44.4 %copy-start.6 = (bf16[128,256]{1,0:T(8,128)(2,1)S(1)}, bf16[128,256]{1,0:T(8,128)(2,1)}, u32[]{:S(2)}) copy-start(bf16[128,256]{1,0:T(8,128)(2,1)} %param.12) | copy-start | bytes 196612
  14.9 93.9 %copy-start.1 = (bf16[1,2,2048,176]{2,3,1,0:T(8,128)(2,1)S(1)}, bf16[1,2,2048,176]{2,3,1,0:T(8,128)(2,1)}, u32[]{:S(2)}) copy-start(bf16[1,2,2048,176]{2,3,1,0:T(8,128)(2,1)} %param.22) | copy-start | bytes 4325380
  57.4 15.0 %copy-start.4 = (bf16[128,256]{1,0:T(8,128)(2,1)}, bf16[128,256]{1,0:T(8,128)(2,1)S(1)}, u32[]{:S(2)}) copy-start(bf16[128,256]{1,0:T(8,128)(2,1)S(1)} %add_convert_fusion) | copy-start | bytes 196612
  58.4 13.8 %all-to-all-start = ((bf16[8,128,256]{1,2,0:T(8,128)(2,1)}), bf16[8,128,256]{1,2,0:T(8,128)(2,1)S(1)}, u32[]{:S(2)}, u32[]{:S(2)}) async-start(bf16[8,128,256]{1,2,0:T(8,128)(2,1)} %stack.2), calls=%async_computation.1 | async-start | bytes 1048576 | tf_op jit(solution)/shard_map/all_to_all | solution.py:81
  61.9 73.7 %all-gather.2.cloned.1.call-start = ((), (), s32[]{:S(2)}) async-start(), calls=%async_computation.6 | async-start | bytes 4718592 | tf_op jit(solution)/shard_map/all_gather | solution.py:109
  110.0 30.5 %copy-start.2 = (bf16[22,8,8,256]{3,2,1,0:T(8,128)(2,1)S(1)}, bf16[22,8,8,256]{3,2,1,0:T(8,128)(2,1)}, u32[]{:S(2)}) copy-start(bf16[22,8,8,256]{3,2,1,0:T(8,128)(2,1)} %copy.129) | copy-start | bytes 2162692
  201.4 15.0 %copy-start.3 = (bf16[2048,64]{0,1:T(8,128)(2,1)S(1)}, bf16[2048,64]{0,1:T(8,128)(2,1)}, u32[]{:S(2)}) copy-start(bf16[2048,64]{0,1:T(8,128)(2,1)} %param.20) | copy-start | bytes 786436
  203.0 42.3 %all-to-all-start.3 = ((f32[64,16,256]{2,1,0:T(8,128)}), f32[64,16,256]{2,1,0:T(8,128)S(1)}, u32[]{:S(2)}, u32[]{:S(2)}) async-start(f32[64,16,256]{2,1,0:T(8,128)} %bitcast.17), calls=%async_computation.4 | async-start | bytes 2097152 | tf_op jit(solution)/shard_map/all_to_all | solution.py:122
Sparse Core Ops, SparseCore 0:
  14.8 41.6 reduce-scatter.1
  106.8 28.8 all-gather.1
